TPU v7x, 256 devices: a whole 4x4x8 slice. The times are simulated.
256 devices in a mesh: grp: 8 (over x, core), seq: 32 (over y, z).
Axes of the slice: x: 4, y: 4, z: 8, core: 2. Of those that a mesh axis runs over, the one named last changes fastest.
Arguments:
- queries: bfloat16 [32768, 512], P(('grp', 'seq')), may hold values from -4.5 to 5.5
- key_vectors: bfloat16 [32768, 512], P(('grp', 'seq')), may hold values from -4.5 to 5.5
- value_vectors: bfloat16 [32768, 1024], P(('grp', 'seq')), may hold values from -6 to 6
- input_gate: float32 [4, 32768], P(None, ('grp', 'seq')), may hold values from -4 to 114
- forget_gate: float32 [4, 32768], P(None, ('grp', 'seq')), may hold values from -3 to 25
Outputs:
- hidden_states: bfloat16 [32768, 1024], P(('grp', 'seq'))
All inputs are finite; a program needn't handle non-finite values.
Results may differ from a plain program's by a relative error of at most 0.028.
Values sent between devices are 32-bit elements; how exact they have to be, the bound alone decides.
A program may use at most 64 MiB of HBM per device.

v0:
```python
import jax
import jax.numpy as jnp
from jax import lax
from jax.sharding import PartitionSpec as P

exact_precision_mode = lax.Precision.HIGHEST
floor_value = -1e30


def prefix_2(value, axis, join, neutral):
    count, mine = (lax.axis_size(axis), lax.axis_index(axis))
    pieces = jax.tree.map(lambda part: lax.all_gather(part, axis), value)
    subtotal = jax.tree.map(
        lambda part, zero: jnp.full_like(part, 0) + jnp.asarray(zero, part.dtype), value, neutral
    )

    def lap(position, subtotal):
        longer = join(subtotal, jax.tree.map(lambda part: part[position], pieces))
        return jax.tree.map(lambda new, old: jnp.where(position < mine, new, old), longer, subtotal)

    return lax.fori_loop(0, count - 1, lap, subtotal)


def broadcast(value, axis, root):
    mine = lax.axis_index(axis) == root
    return lax.psum(jnp.where(mine, value, jnp.zeros_like(value)), axis)


def combine_states(earlier, later):
    early_matrix, early_vector, early_top, early_decay = earlier
    late_matrix, late_vector, late_top, late_decay = later
    joined = jnp.maximum(early_top + late_decay, late_top)
    early_weight = jnp.exp(early_top + late_decay - joined)
    late_weight = jnp.exp(late_top - joined)
    new_matrix = (
        early_weight[..., None, None] * early_matrix + late_weight[..., None, None] * late_matrix
    )
    new_vector = early_weight[..., None] * early_vector + late_weight[..., None] * late_vector
    return (new_matrix, new_vector, joined, early_decay + late_decay)


def on_device(queries, key_vectors, value_vectors, input_gate, forget_gate):
    head_count = input_gate.shape[0]
    length = queries.shape[0]
    key_dim = queries.shape[1] // head_count
    value_dim = value_vectors.shape[1] // head_count
    query_scaling = key_dim ** (-0.5)
    cumulative = jnp.cumsum(jax.nn.log_sigmoid(forget_gate), axis=1)
    block_decay = cumulative[:, -1]
    weight_log = block_decay[:, None] - cumulative + input_gate
    block_top = jnp.max(weight_log, axis=1)
    weight_tensor = jnp.exp(weight_log - block_top[:, None])
    keys_widened = key_vectors.astype(jnp.float32).reshape(length, head_count, key_dim)
    values_widened = (
        value_vectors.astype(jnp.float32).reshape(length, head_count, value_dim)
        * weight_tensor.T[:, :, None]
    )
    memory_matrix = jnp.einsum(
        "fji,fjb->jib", keys_widened, values_widened, precision=exact_precision_mode
    )
    vector = jnp.einsum("shk,hs->hk", keys_widened, weight_tensor, precision=exact_precision_mode)
    local_state = (memory_matrix, vector, block_top, block_decay)
    identity = (
        jnp.zeros_like(memory_matrix),
        jnp.zeros_like(vector),
        jnp.full_like(block_top, floor_value),
        jnp.zeros_like(block_decay),
    )
    within = prefix_2(local_state, "seq", combine_states, identity)
    through = combine_states(within, local_state)
    group_state = (
        broadcast(through[0], "seq", lax.axis_size("seq") - 1),
        broadcast(through[1], "seq", lax.axis_size("seq") - 1),
        broadcast(through[2], "seq", lax.axis_size("seq") - 1),
        broadcast(through[3], "seq", lax.axis_size("seq") - 1),
    )
    before = prefix_2(group_state, "grp", combine_states, identity)
    prefix = combine_states(before, within)
    previous_memory_matrix, prev_vector, prev_top, prev_decay = prefix
    rows = lax.broadcasted_iota(jnp.int32, (length, length), 0)
    cols = lax.broadcasted_iota(jnp.int32, (length, length), 1)
    causal = rows >= cols
    pieces = []
    for head_index in range(head_count):
        query_head = queries[:, head_index * key_dim : (head_index + 1) * key_dim]
        key_head = key_vectors[:, head_index * key_dim : (head_index + 1) * key_dim]
        value_head = value_vectors[:, head_index * value_dim : (head_index + 1) * value_dim]
        scores = (
            jnp.einsum("tk,sk->ts", query_head, key_head, preferred_element_type=jnp.float32)
            * query_scaling
        )
        head_cumul = cumulative[head_index]
        log_decay = head_cumul[:, None] - head_cumul[None, :] + input_gate[head_index][None, :]
        log_decay = jnp.where(causal, log_decay, -jnp.inf)
        row_top = jnp.max(log_decay, axis=1)
        weighted = jnp.exp(log_decay - row_top[:, None]) * scores
        inner_den = jnp.sum(weighted, axis=1)
        inner_num = jnp.dot(
            weighted.astype(jnp.bfloat16), value_head, preferred_element_type=jnp.float32
        )
        head_top = prev_top[head_index]
        stab = jnp.maximum(head_cumul + head_top, row_top)
        inner_factor = jnp.exp(row_top - stab)
        outer_factor = jnp.exp(head_cumul + head_top - stab)
        query_widened = query_head.astype(jnp.float32)
        carried_numerator = (
            jnp.dot(
                query_widened, previous_memory_matrix[head_index], precision=exact_precision_mode
            )
            * query_scaling
        )
        carried_den = (
            jnp.dot(query_widened, prev_vector[head_index], precision=exact_precision_mode)
            * query_scaling
        )
        numer = inner_factor[:, None] * inner_num + outer_factor[:, None] * carried_numerator
        denom = inner_factor * inner_den + outer_factor * carried_den
        output = numer / jnp.maximum(jnp.abs(denom), jnp.exp(-stab))[:, None]
        pieces.append(output.astype(jnp.bfloat16))
    return jnp.concatenate(pieces, axis=1)


def solution(mesh):
    return jax.shard_map(
        on_device,
        mesh=mesh,
        in_specs=(
            P(("grp", "seq"), None),
            P(("grp", "seq"), None),
            P(("grp", "seq"), None),
            P(None, ("grp", "seq")),
            P(None, ("grp", "seq")),
        ),
        out_specs=P(("grp", "seq"), None),
        check_vma=False,
    )
```

profile of v0, /device:TPU:32, one launch (start us, length us, event | category | flops | bytes accessed | tf_op | source)
XLA Modules:
  0.0 472.3 jit_solution(16143774896699042304)
XLA Ops:
  10.6 1.3 convolution_bitcast_fusion
  13.0 1.3 dynamic-slice
  15.3 74.9 %all-reduce.3 = (f32[128]{0:T(128)S(1)}, f32[128]{0:T(128)S(1)}) all-reduce(f32[128]{0:T(128)S(1)} %dynamic-update-slice, f32[128]{0:T(128)S(1)} %dynamic-update-slice.1), channel_id=2, replica_groups=mesh['grp'=8,'seq'=32] {'seq'}, use_global_device_ids=true, to_apply=%add | all-reduce | flops 256 | bytes 2048
  91.6 51.7 %all-gather.4 = f32[32,4,128]{2,1,0:T(4,128)S(1)} all-gather(f32[1,4,128]{2,1,0:T(4,128)S(1)} %bitcast.266), channel_id=5, replica_groups=mesh['grp'=8,'seq'=32] {'seq'}, dimensions={0}, use_global_device_ids=true | all-gather | bytes 67584 | tf_op jit(solution)/shard_map/all_gather | solution.py:12
  143.3 10.9 %all-gather.12.cloned.1.call-done = f32[128,128,256]{2,1,0:T(8,128)} async-done(((f32[4,128,256]{2,1,0:T(8,128)}), f32[128,128,256]{2,1,0:T(8,128)}) %all-gather.12.cloned.1.call-update) | async-done | bytes 16777232 | tf_op jit(solution)/shard_map/all_gather | solution.py:12
  154.3 40.9 %while.38 = (s32[]{:T(128)}, f32[4,128,256]{2,1,0:T(8,128)S(1)}, f32[4,128]{1,0:T(4,128)S(1)}, f32[4]{0:T(128)S(1)}, f32[4]{0:T(128)S(1)}, /*index=5*/s32[]{:T(1...) while((s32[]{:T(128)}, f32[4,128,256]{2,1,0:T(8,128)S(1)}, ...), condition=%wide.region_4.5_spmd.clone, body=%wide.region_3.4_spmd.clone.sunk | while | flops 657964 | bytes 1579405 | solution.py:21
  154.3 1.2 fusion.119
  155.6 1.2 fusion.119
  156.9 1.2 fusion.119
  158.3 1.2 fusion.119
  159.6 1.2 fusion.119
  160.9 1.2 fusion.119
  162.2 1.2 fusion.119
  163.5 1.2 fusion.119
  164.8 1.2 fusion.119
  166.2 1.2 fusion.119
  167.5 1.2 fusion.119
  168.8 1.2 fusion.119
  170.1 1.2 fusion.119
  171.4 1.2 fusion.119
  172.8 1.2 fusion.119
  174.1 1.2 fusion.119
  175.4 1.2 fusion.119
  176.7 1.2 fusion.119
  178.0 1.2 fusion.119
  179.4 1.2 fusion.119
  180.7 1.2 fusion.119
  182.0 1.2 fusion.119
  183.3 1.2 fusion.119
  184.6 1.2 fusion.119
  185.9 1.2 fusion.119
  187.3 1.2 fusion.119
  188.6 1.2 fusion.119
  189.9 1.2 fusion.119
  191.2 1.2 fusion.119
  192.5 1.2 fusion.119
  193.9 1.2 fusion.119
  196.4 147.1 %all-reduce.6.cloned.1.call-done = f32[1,4,128,256]{2,3,1,0:T(8,128)} async-done(((f32[1,4,128,256]{2,3,1,0:T(8,128)}), f32[1,4,128,256]{2,3,1,0:T(8,128)}) %all-reduce.6.cloned.1.call-update) | async-done | bytes 524304 | tf_op jit(solution)/shard_map/psum | solution.py:26
  343.5 2.0 copy.38
  346.7 70.8 %all-reduce.2 = (f32[1,4]{1,0:T(1,128)S(1)}, f32[1,4]{1,0:T(1,128)S(1)}, f32[1,4,128]{2,1,0:T(4,128)S(1)}) all-reduce(f32[1,4]{1,0:T(1,128)S(1)} %get-tuple-element.533, f32[1,4]{1,0:T(1,128)S(1)} %get-tuple-element.528, f32[1,4,128]{2,1,0:T(4,128)S(1)} %select_bitcast_fusion.1), channel_id=1, replica_groups=mesh['grp'=8,'seq'=32] {'seq'}, use_global_device_ids=true, to_apply=%region_8.9 | all-reduce | flops 520 | bytes 4160 | tf_op jit(solution)/shard_map/psum | solution.py:26
  417.6 10.5 %all-gather.5 = f32[8,1,4]{2,1,0:T(1,128)S(1)} all-gather(f32[1,1,4]{2,1,0:T(1,128)S(1)} %bitcast.270), channel_id=1, replica_groups=mesh['grp'=8,'seq'=32] {'grp'}, dimensions={0}, use_global_device_ids=true | all-gather | bytes 144 | tf_op jit(solution)/shard_map/all_gather | solution.py:12
  428.0 8.1 %all-gather.6 = f32[8,1,4]{2,1,0:T(1,128)S(1)} all-gather(f32[1,1,4]{2,1,0:T(1,128)S(1)} %bitcast.269), channel_id=1, replica_groups=mesh['grp'=8,'seq'=32] {'grp'}, dimensions={0}, use_global_device_ids=true | all-gather | bytes 144 | tf_op jit(solution)/shard_map/all_gather | solution.py:12
  436.2 11.3 %all_gather.59 = f32[8,4,128]{2,1,0:T(4,128)S(1)} all-gather(f32[1,4,128]{2,1,0:T(4,128)S(1)} %get-tuple-element.490), channel_id=1, replica_groups=mesh['grp'=8,'seq'=32] {'grp'}, dimensions={0}, use_global_device_ids=true | all-gather | bytes 18432 | tf_op jit(solution)/shard_map/all_gather | solution.py:12
  447.5 9.2 %while.39 = (s32[]{:T(128)}, f32[4,128,256]{2,1,0:T(8,128)S(1)}, f32[4,128]{1,0:T(4,128)S(1)}, f32[4]{0:T(128)S(1)}, s32[]{:T(128)}, /*index=5*/f32[8,4]{1,0:T(8...) while((s32[]{:T(128)}, f32[4,128,256]{2,1,0:T(8,128)S(1)}, ...), condition=%wide.region_10.11_spmd.clone, body=%wide.region_9.10_spmd.clone.sunk | while | flops 657952 | bytes 1579365 | solution.py:21
  447.5 1.2 fusion.121
  448.8 1.2 fusion.121
  452.7 1.2 fusion.121
  459.0 2.6 broadcast_multiply_fusion.3
  (184 shorter events, 24.9 us)
Async XLA Ops:
  6.5 339.0 %copy-start.2 = (f32[4,128]{1,0:T(4,128)S(1)}, f32[4,128]{1,0:T(4,128)}, u32[]{:S(2)}) copy-start(f32[4,128]{1,0:T(4,128)} %param.12) | copy-start | bytes 6148
  6.5 456.8 %copy-start = (bf16[128,1024]{1,0:T(8,128)(2,1)S(1)}, bf16[128,1024]{1,0:T(8,128)(2,1)}, u32[]{:S(2)}) copy-start(bf16[128,1024]{1,0:T(8,128)(2,1)} %param.11) | copy-start | bytes 786436
  6.5 339.4 %copy-start.1 = (bf16[128,512]{1,0:T(8,128)(2,1)S(1)}, bf16[128,512]{1,0:T(8,128)(2,1)}, u32[]{:S(2)}) copy-start(bf16[128,512]{1,0:T(8,128)(2,1)} %param.10) | copy-start | bytes 393220
  6.5 339.4 %copy-start.3 = (bf16[128,512]{1,0:T(8,128)(2,1)S(1)}, bf16[128,512]{1,0:T(8,128)(2,1)}, u32[]{:S(2)}) copy-start(bf16[128,512]{1,0:T(8,128)(2,1)} %param.9) | copy-start | bytes 393220
  6.5 147.7 %all-gather.12.cloned.1.call-start = ((), (), s32[]{:S(2)}) async-start(), calls=%async_computation.2 | async-start | bytes 17301504 | tf_op jit(solution)/shard_map/all_gather | solution.py:12
  12.9 330.6 %all-reduce.6.cloned.1.call-start = ((), (), s32[]{:S(2)}) async-start(), calls=%async_computation | async-start | bytes 1048576 | tf_op jit(solution)/shard_map/psum | solution.py:26
  196.3 251.1 %all-gather.10.cloned.1.call-start = ((), (), s32[]{:S(2)}) async-start(), calls=%async_computation.1 | async-start | bytes 4718592 | tf_op jit(solution)/shard_map/all_gather | solution.py:12
Sparse Core Ops, SparseCore 0:
  13.0 141.2 all-gather.11
  196.5 146.9 all-reduce.5
  345.7 32.3 all-gather.9
where the time goes:
time: 479 us; the launch traced here: 472 us
  blocking collectives  227 us (47%)
  waiting for transfers between devices  158 us (33%)
  other arithmetic  57.3 us (12%)
  between operations  14 us (3%)
  matrix products  8.03 us (2%)
  local copies, waits for them, and re-layouts  7.09 us (1%)
    psum x1, waiting for transfers between devices, broadcast(): return lax.psum(jnp.where(mine, value, jnp.zeros_like(value)), axis)  147 us
    all_gather x4, blocking collectives, prefix_2(): pieces = jax.tree.map(lambda part: lax.all_gather(part, axis), value)  81.6 us
    unnamed x1, blocking collectives  74.9 us
    psum x1, blocking collectives, broadcast(): return lax.psum(jnp.where(mine, value, jnp.zeros_like(value)), axis)  70.8 us
    select_n x114, other arithmetic, lap(): jnp.where(position < mine, new, old)  49.2 us
    all_gather x2, waiting for transfers between devices, prefix_2(): pieces = jax.tree.map(lambda part: lax.all_gather(part, axis), value)  10.9 us
  transfers between devices with their start and end apart: 3, of which 2 were waited for; matrix products, arithmetic and copies ran while one was open for 1% of the time, Pallas kernels for 0%

commit v1 on v0

v1 whole, which is shorter than its diff:
```python
import functools

import jax
import jax.numpy as jnp
from jax import lax
from jax.experimental import pallas as pl
from jax.experimental.pallas import tpu as pltpu
from jax.sharding import PartitionSpec as P

MESH = pl.DeviceIdType.MESH
FLOOR = -1e30
CHUNKS = 1
EXACT = lax.Precision.HIGHEST


def split3(x):
    hi = x.astype(jnp.bfloat16)
    rest = x - hi.astype(jnp.float32)
    mid = rest.astype(jnp.bfloat16)
    low = (rest - mid.astype(jnp.float32)).astype(jnp.bfloat16)
    return hi, mid, low


def kernel(
    ng, ns, heads, kd, vd, length,
    q_hbm, k_hbm, v_hbm, ig_ref, fg_ref, o_ref,
    qv, kv, vv, state, inner, rbuf, pbuf, pfull, scal, rscal, gsend, grecv, gscal, grscal,
    acoef, bcoef, tops, decs, nbuf,
    in_sem, s1, r1, ss, rs, sg, rg, sgs, rgs, s3, r3,
):
    hc = heads // CHUNKS
    rp = kd * (vd // 128) // ns
    cols = vd // 128
    scale = kd ** (-0.5)
    myg = lax.axis_index("grp")
    me = lax.axis_index("seq")

    def seq_peer(d):
        return lax.rem(me + d, ns)

    def grp_peer(d):
        return lax.rem(myg + d, ng)

    copies = [
        pltpu.make_async_copy(src, dst, in_sem.at[n])
        for n, (src, dst) in enumerate(((k_hbm, kv), (v_hbm, vv), (q_hbm, qv)))
    ]
    for copy in copies:
        copy.start()

    barrier = pltpu.get_barrier_semaphore()

    @pl.loop(1, ns)
    def _(d):
        pl.semaphore_signal(barrier, inc=1, device_id=(myg, seq_peer(d)), device_id_type=MESH)

    @pl.loop(1, ng)
    def _(d):
        pl.semaphore_signal(barrier, inc=1, device_id=(grp_peer(d), me), device_id_type=MESH)

    lane = lax.broadcasted_iota(jnp.int32, (heads, 128), 1)
    rows = lax.broadcasted_iota(jnp.int32, (length, length), 0)
    lanes = lax.broadcasted_iota(jnp.int32, (length, length), 1)

    def pack(left, right):
        return jnp.where(lane < 64, left, right)

    def unpack(row):
        turned = pltpu.roll(row, 64, 1)
        return jnp.where(lane < 64, row, turned), jnp.where(lane < 64, turned, row)

    forget = fg_ref[...]
    gate = ig_ref[...]
    logf = jnp.minimum(forget, 0.0) - jnp.log1p(jnp.exp(-jnp.abs(forget)))
    upper = jnp.where(rows <= lanes, 1.0, 0.0)
    cumul = jnp.dot(logf, upper, precision=EXACT, preferred_element_type=jnp.float32)
    decay = jnp.sum(jnp.where(lane == length - 1, cumul, 0.0), axis=1, keepdims=True)
    level = gate - cumul
    wlog = decay + level
    top = jnp.max(wlog, axis=1, keepdims=True)
    weight = jnp.exp(wlog - top)
    decay_row = jnp.broadcast_to(decay, (heads, 128))
    top_row = jnp.broadcast_to(top, (heads, 128))

    copies[0].wait()
    hi, mid, low = split3(weight)
    lhs = jnp.concatenate([hi, mid, low, jnp.zeros_like(low)], axis=0)
    for h in range(heads):
        part = jnp.dot(lhs, kv[:, h * kd : (h + 1) * kd], preferred_element_type=jnp.float32)
        scal[h : h + 1, :] = (
            part[h : h + 1] + part[heads + h : heads + h + 1] + part[2 * heads + h : 2 * heads + h + 1]
        )
    scal[heads : 2 * heads, :] = pack(decay_row, top_row)
    rscal[me] = scal[...]

    pl.semaphore_wait(barrier, ns - 1 + ng - 1)

    def scal_copy(d):
        return pltpu.make_async_remote_copy(
            src_ref=scal, dst_ref=rscal.at[me], send_sem=ss.at[d], recv_sem=rs.at[me],
            device_id=(myg, seq_peer(d)), device_id_type=MESH,
        )

    @pl.loop(1, ns)
    def _(d):
        scal_copy(d).start()

    copies[1].wait()

    def slice_of(ref, c, o):
        row = pl.multiple_of(lax.div(o, cols) * rp, 8)
        col = pl.multiple_of(lax.rem(o, cols) * 128, 128)
        return ref.at[pl.ds(c * hc, hc), pl.ds(row, rp), pl.ds(col, 128)]

    def state_copy(c, d):
        o = seq_peer(d)
        return pltpu.make_async_remote_copy(
            src_ref=slice_of(state, c, o), dst_ref=rbuf.at[me, pl.ds(c * hc, hc)],
            send_sem=s1.at[c, d], recv_sem=r1.at[c, me], device_id=(myg, o), device_id_type=MESH,
        )

    for c in range(CHUNKS):
        for h in range(c * hc, (c + 1) * hc):
            turned = kv[:, h * kd : (h + 1) * kd].astype(jnp.float32).T
            scaled = (turned * weight[h : h + 1, :]).astype(jnp.bfloat16)
            state[h] = jnp.dot(
                scaled, vv[:, h * vd : (h + 1) * vd], preferred_element_type=jnp.float32
            )

        @pl.loop(1, ns)
        def _(d, c=c):
            state_copy(c, d).start()

        rbuf[me, c * hc : (c + 1) * hc] = slice_of(state, c, me)[...]

    copies[2].wait()
    columns = []
    for h in range(heads):
        scores = scale * lax.dot_general(
            qv[:, h * kd : (h + 1) * kd], kv[:, h * kd : (h + 1) * kd],
            (((1,), (1,)), ((), ())), preferred_element_type=jnp.float32,
        )
        masked = jnp.where(rows >= lanes, level[h : h + 1, :], -jnp.inf)
        reach = jnp.max(masked, axis=1, keepdims=True)
        weighted = jnp.exp(masked - reach) * scores
        inner_den = jnp.sum(weighted, axis=1, keepdims=True)
        cumul_col = jnp.sum(
            jnp.where(rows == lanes, cumul[h : h + 1, :], 0.0), axis=1, keepdims=True
        )
        inner[h] = jnp.dot(
            weighted.astype(jnp.bfloat16), vv[:, h * vd : (h + 1) * vd],
            preferred_element_type=jnp.float32,
        )
        columns.append((reach, inner_den, cumul_col))

    @pl.loop(1, ns)
    def _(d):
        src = seq_peer(d)
        pltpu.make_async_remote_copy(
            src_ref=scal, dst_ref=rscal.at[src], send_sem=ss.at[d], recv_sem=rs.at[src],
            device_id=(myg, src), device_id_type=MESH,
        ).wait_recv()

    run_top = jnp.full((heads, 128), FLOOR, jnp.float32)
    run_dec = jnp.zeros((heads, 128), jnp.float32)
    run_vec = jnp.zeros((heads, 128), jnp.float32)
    for i in range(ns):
        dec_i, top_i = unpack(rscal[i, heads : 2 * heads, :])
        tops[i] = run_top
        decs[i] = run_dec
        nbuf[i] = run_vec
        early = run_top + dec_i
        joined = jnp.maximum(early, top_i)
        a = jnp.exp(early - joined)
        b = jnp.exp(top_i - joined)
        acoef[i] = a
        bcoef[i] = b
        run_vec = a * run_vec + b * rscal[i, 0:heads, :]
        run_top = joined
        run_dec = run_dec + dec_i
    gscal[0:heads, :] = run_vec
    gscal[heads : 2 * heads, :] = pack(run_dec, run_top)
    grscal[myg] = gscal[...]

    @pl.loop(1, ng)
    def _(d):
        pltpu.make_async_remote_copy(
            src_ref=gscal, dst_ref=grscal.at[myg], send_sem=sgs.at[d], recv_sem=rgs.at[myg],
            device_id=(grp_peer(d), me), device_id_type=MESH,
        ).start()

    for c in range(CHUNKS):
        @pl.loop(1, ns)
        def _(d, c=c):
            src = seq_peer(d)
            pltpu.make_async_remote_copy(
                src_ref=slice_of(state, c, src), dst_ref=rbuf.at[src, pl.ds(c * hc, hc)],
                send_sem=s1.at[c, d], recv_sem=r1.at[c, src], device_id=(myg, src), device_id_type=MESH,
            ).wait_recv()

        for h in range(c * hc, (c + 1) * hc):
            run = jnp.zeros((rp, 128), jnp.float32)
            for i in range(ns):
                pbuf[i, h] = run
                run = acoef[i, h : h + 1, :] * run + bcoef[i, h : h + 1, :] * rbuf[i, h]
            gsend[h] = run
        grecv[myg, c * hc : (c + 1) * hc] = gsend[c * hc : (c + 1) * hc]

        @pl.loop(1, ng)
        def _(d, c=c):
            pltpu.make_async_remote_copy(
                src_ref=gsend.at[pl.ds(c * hc, hc)], dst_ref=grecv.at[myg, pl.ds(c * hc, hc)],
                send_sem=sg.at[c, d], recv_sem=rg.at[c, myg], device_id=(grp_peer(d), me), device_id_type=MESH,
            ).start()

    @pl.loop(1, ng)
    def _(d):
        src = grp_peer(d)
        pltpu.make_async_remote_copy(
            src_ref=gscal, dst_ref=grscal.at[src], send_sem=sgs.at[d], recv_sem=rgs.at[src],
            device_id=(src, me), device_id_type=MESH,
        ).wait_recv()

    before_top = jnp.full((heads, 128), FLOOR, jnp.float32)
    before_vec = jnp.zeros((heads, 128), jnp.float32)
    weights = []
    for g in range(ng):
        dec_g, top_g = unpack(grscal[g, heads : 2 * heads, :])
        counts = g < myg
        early = before_top + dec_g
        joined = jnp.maximum(early, top_g)
        a = jnp.where(counts, jnp.exp(early - joined), 1.0)
        b = jnp.where(counts, jnp.exp(top_g - joined), 0.0)
        before_vec = a * before_vec + b * grscal[g, 0:heads, :]
        before_top = jnp.where(counts, joined, before_top)
        weights.append((a, b))

    for i in range(ns):
        early = before_top + decs[i]
        full = jnp.maximum(early, tops[i])
        acoef[i] = jnp.exp(early - full)
        bcoef[i] = jnp.exp(tops[i] - full)
        tops[i] = full
    prev_top = tops[me]
    prev_vec = acoef[me] * before_vec + bcoef[me] * nbuf[me]

    def back_copy(c, d, src):
        o = seq_peer(d)
        return pltpu.make_async_remote_copy(
            src_ref=pbuf.at[o, pl.ds(c * hc, hc)], dst_ref=slice_of(pfull, c, src),
            send_sem=s3.at[c, d], recv_sem=r3.at[c, src], device_id=(myg, o), device_id_type=MESH,
        )

    for c in range(CHUNKS):
        @pl.loop(1, ng)
        def _(d, c=c):
            src = grp_peer(d)
            pltpu.make_async_remote_copy(
                src_ref=gsend.at[pl.ds(c * hc, hc)], dst_ref=grecv.at[src, pl.ds(c * hc, hc)],
                send_sem=sg.at[c, d], recv_sem=rg.at[c, src], device_id=(src, me), device_id_type=MESH,
            ).wait_recv()

        for h in range(c * hc, (c + 1) * hc):
            run = jnp.zeros((rp, 128), jnp.float32)
            for g in range(ng):
                a, b = weights[g]
                run = a[h : h + 1, :] * run + b[h : h + 1, :] * grecv[g, h]
            for i in range(ns):
                pbuf[i, h] = acoef[i, h : h + 1, :] * run + bcoef[i, h : h + 1, :] * pbuf[i, h]

        @pl.loop(1, ns)
        def _(d, c=c):
            back_copy(c, d, me).start()

        slice_of(pfull, c, me)[...] = pbuf[me, c * hc : (c + 1) * hc]

    for c in range(CHUNKS):
        @pl.loop(1, ns)
        def _(d, c=c):
            back_copy(c, d, seq_peer(d)).wait_recv()

        for h in range(c * hc, (c + 1) * hc):
            reach, inner_den, cumul_col = columns[h]
            query = qv[:, h * kd : (h + 1) * kd]
            carried = scale * jnp.dot(
                query, pfull[h].astype(jnp.bfloat16), preferred_element_type=jnp.float32
            )
            carried_den = scale * jnp.sum(
                query.astype(jnp.float32) * prev_vec[h : h + 1, :], axis=1, keepdims=True
            )
            prev = jnp.max(prev_top[h : h + 1, :], axis=1, keepdims=True)
            peak = jnp.maximum(prev, reach)
            inner_factor = jnp.exp(reach - peak)
            outer_factor = jnp.exp(prev - peak)
            denom = inner_factor * inner_den + outer_factor * carried_den
            bound = jnp.maximum(jnp.abs(denom), jnp.exp(-(cumul_col + peak)))
            numer = inner_factor * inner[h] + outer_factor * carried
            o_ref[:, h * vd : (h + 1) * vd] = (numer / bound).astype(jnp.bfloat16)

    @pl.loop(1, ns)
    def _(d):
        scal_copy(d).wait_send()
        for c in range(CHUNKS):
            state_copy(c, d).wait_send()
            back_copy(c, d, me).wait_send()

    @pl.loop(1, ng)
    def _(d):
        pltpu.make_async_remote_copy(
            src_ref=gscal, dst_ref=grscal.at[myg], send_sem=sgs.at[d], recv_sem=rgs.at[myg],
            device_id=(grp_peer(d), me), device_id_type=MESH,
        ).wait_send()
        for c in range(CHUNKS):
            pltpu.make_async_remote_copy(
                src_ref=gsend.at[pl.ds(c * hc, hc)], dst_ref=grecv.at[myg, pl.ds(c * hc, hc)],
                send_sem=sg.at[c, d], recv_sem=rg.at[c, myg], device_id=(grp_peer(d), me), device_id_type=MESH,
            ).wait_send()


def on_device(ng, ns, queries, key_vectors, value_vectors, input_gate, forget_gate):
    heads, length = input_gate.shape
    kd = queries.shape[1] // heads
    vd = value_vectors.shape[1] // heads
    rp = kd * (vd // 128) // ns
    f32 = jnp.float32
    dma = pltpu.SemaphoreType.DMA
    vmem = pl.BlockSpec(memory_space=pltpu.VMEM)
    hbm = pl.BlockSpec(memory_space=pl.ANY)
    return pl.pallas_call(
        functools.partial(kernel, ng, ns, heads, kd, vd, length),
        out_shape=jax.ShapeDtypeStruct(value_vectors.shape, jnp.bfloat16),
        in_specs=[hbm, hbm, hbm, vmem, vmem],
        out_specs=vmem,
        scratch_shapes=[
            pltpu.VMEM(queries.shape, jnp.bfloat16),
            pltpu.VMEM(key_vectors.shape, jnp.bfloat16),
            pltpu.VMEM(value_vectors.shape, jnp.bfloat16),
            pltpu.VMEM((heads, kd, vd), f32),
            pltpu.VMEM((heads, length, vd), f32),
            pltpu.VMEM((ns, heads, rp, 128), f32),
            pltpu.VMEM((ns, heads, rp, 128), f32),
            pltpu.VMEM((heads, kd, vd), f32),
            pltpu.VMEM((2 * heads, 128), f32),
            pltpu.VMEM((ns, 2 * heads, 128), f32),
            pltpu.VMEM((heads, rp, 128), f32),
            pltpu.VMEM((ng, heads, rp, 128), f32),
            pltpu.VMEM((2 * heads, 128), f32),
            pltpu.VMEM((ng, 2 * heads, 128), f32),
            pltpu.VMEM((ns, heads, 128), f32),
            pltpu.VMEM((ns, heads, 128), f32),
            pltpu.VMEM((ns, heads, 128), f32),
            pltpu.VMEM((ns, heads, 128), f32),
            pltpu.VMEM((ns, heads, 128), f32),
            dma((3,)),
            dma((CHUNKS, ns)), dma((CHUNKS, ns)),
            dma((ns,)), dma((ns,)),
            dma((CHUNKS, ng)), dma((CHUNKS, ng)),
            dma((ng,)), dma((ng,)),
            dma((CHUNKS, ns)), dma((CHUNKS, ns)),
        ],
        compiler_params=pltpu.CompilerParams(collective_id=0, has_side_effects=True),
        name="mlstm_layer",
    )(queries, key_vectors, value_vectors, input_gate, forget_gate)


def solution(mesh):
    return jax.shard_map(
        functools.partial(on_device, mesh.shape["grp"], mesh.shape["seq"]),
        mesh=mesh,
        in_specs=(
            P(("grp", "seq"), None),
            P(("grp", "seq"), None),
            P(("grp", "seq"), None),
            P(None, ("grp", "seq")),
            P(None, ("grp", "seq")),
        ),
        out_specs=P(("grp", "seq"), None),
        check_vma=False,
    )
```

time: 479 us -> 53.7 us (0.11)
  the two profiles are of different devices: /device:TPU:32 before, /device:TPU:1 now
where the time goes in v1:
time: 53.7 us; the launch traced here: 53.5 us
  Pallas kernels  51.8 us (96%)
  local copies, waits for them, and re-layouts  1.67 us (3%)
    pallas_call x1, Pallas kernels, on_device(): pl.pallas_call(functools.partial(kernel, ng, ns, heads, kd, vd, length),...  51.8 us
    unnamed x1, local copies, waits for them, and re-layouts  1.67 us

profile of v1, /device:TPU:1, one launch (start us, length us, event | category | flops | bytes accessed | tf_op | source)
XLA Modules:
  0.0 53.5 jit_solution(13841779831400530171)
XLA Ops:
  0.0 51.8 %mlstm_layer.1 = bf16[128,1024]{1,0:T(8,128)(2,1)} custom-call(bf16[128,512]{1,0:T(8,128)(2,1)} %q_hbm.1, bf16[128,512]{1,0:T(8,128)(2,1)} %k_hbm.1, bf16[128,1024]{1,0:T(8,128)(2,1)} %v_hbm.1, f32[4,128]{1,0:T(4,128)} %ig_ref.1, f32[4,128]{1,0:T(4,128)} %fg_ref.1), custom_call_target="tpu_custom_call" | custom-call | tf_op jit(solution)/shard_map/mlstm_layer/pallas_call | solution.py:329
  51.9 1.7 %copy.7 = bf16[128,1024]{1,0:T(8,128)(2,1)} copy(bf16[128,1024]{1,0:T(8,128)(2,1)} %mlstm_layer.1) | data formatting | bytes 524288

commit v2 on v1

v2 whole, which is shorter than its diff:
```python
import functools

import jax
import jax.numpy as jnp
from jax import lax
from jax.experimental import pallas as pl
from jax.experimental.pallas import tpu as pltpu
from jax.sharding import PartitionSpec as P

MESH = pl.DeviceIdType.MESH
FLOOR = -1e30
CHUNKS = 2
BACK = 1
ORDER = 1
UP = 1
EARLY = 1


def split3(x):
    hi = x.astype(jnp.bfloat16)
    rest = x - hi.astype(jnp.float32)
    mid = rest.astype(jnp.bfloat16)
    low = (rest - mid.astype(jnp.float32)).astype(jnp.bfloat16)
    return hi, mid, low


def kernel(
    ng, ns, heads, kd, vd, length,
    q_hbm, k_hbm, v_hbm, ig_hbm, fg_hbm, o_ref,
    ig, fg, qv, kv, vv, state, inner, rbuf, pbuf, pfull, gsend, grecv,
    small, rsmall, gsmall, grsmall, vec, rvec, gvec, grvec, nback, rnback, nrows,
    rows_a, rows_b, rows_t, rows_d, wide_a, wide_b, wide_c, wide_d, group_a, group_b, group_wide_a, group_wide_b,
    in_sem, s1, r1, ss, rs, sg, rg, sgs, rgs, s3, r3, sn, rn, sv, rv, sgv, rgv,
):
    f32, bf16 = jnp.float32, jnp.bfloat16
    hc = heads // CHUNKS
    rp = kd * (vd // 128) // ns
    cols = vd // 128
    ydim = max(1, ns // 8)
    zdim = ns // ydim
    per_head = ns // heads
    span = 64 // heads
    scale = kd ** (-0.5)
    myg = lax.axis_index("grp")
    me = lax.axis_index("seq")
    myh = lax.div(me, per_head)
    owns_vector = lax.rem(me, per_head) == 0

    def seq_peer(d):
        return lax.rem(me + d, ns)

    def grp_peer(d):
        return lax.rem(myg + d, ng)

    copies = [
        pltpu.make_async_copy(src, dst, in_sem.at[n])
        for n, (src, dst) in enumerate(
            ((fg_hbm, fg), (ig_hbm, ig), (k_hbm, kv), (v_hbm, vv), (q_hbm, qv))
        )
    ]
    for copy in copies:
        copy.start()

    barrier = pltpu.get_barrier_semaphore()
    zero = jnp.zeros((1, 128), f32)
    if UP:
        for g in range(ng):
            grsmall[g] = zero
            grvec[g] = zero
            for h in range(heads):
                grecv[g, h] = jnp.zeros((rp, 128), f32)

    @pl.loop(1, ns)
    def _(d):
        pl.semaphore_signal(barrier, inc=1, device_id=(myg, seq_peer(d)), device_id_type=MESH)

    @pl.loop(1, ng)
    def _(d):
        pl.semaphore_signal(barrier, inc=1, device_id=(grp_peer(d), me), device_id_type=MESH)

    lane = lax.broadcasted_iota(jnp.int32, (heads, 128), 1)
    head_row = lax.broadcasted_iota(jnp.int32, (heads, 128), 0)
    rows = lax.broadcasted_iota(jnp.int32, (length, length), 0)
    lanes = lax.broadcasted_iota(jnp.int32, (length, length), 1)

    def slice_of(ref, c, o):
        row = pl.multiple_of(lax.div(o, cols) * rp, 8)
        col = pl.multiple_of(lax.rem(o, cols) * 128, 128)
        return ref.at[pl.ds(c * hc, hc), pl.ds(row, rp), pl.ds(col, 128)]

    def part(c):
        return pl.ds(c * hc, hc)

    def remote(src, dst, send, recv, device):
        return pltpu.make_async_remote_copy(
            src_ref=src, dst_ref=dst, send_sem=send, recv_sem=recv, device_id=device, device_id_type=MESH
        )

    def small_copy(o, slot):
        return remote(
            small, rsmall.at[slot], ss.at[o], rs.at[slot], (myg, o)
        )

    def block_vector_copy(h, o, slot):
        return remote(vec.at[h], rvec.at[slot], sv.at[h], rv.at[slot], (myg, o))

    def group_vector_copy(o, slot):
        return remote(gvec, grvec.at[slot], sgv.at[o], rgv.at[slot], (o, me))

    def state_copy(c, o, slot):
        return remote(
            slice_of(state, c, o), rbuf.at[slot, part(c)], s1.at[c, o], r1.at[c, slot], (myg, o)
        )

    def back_copy(c, o, slot):
        return remote(
            pbuf.at[o, part(c)], slice_of(pfull, c, slot), s3.at[c, o], r3.at[c, slot], (myg, o)
        )

    def vector_copy(o, h):
        return remote(nback.at[o], rnback.at[h], sn.at[o], rn.at[h], (myg, o))

    def group_small_copy(o, slot):
        return remote(gsmall, grsmall.at[slot], sgs.at[o], rgs.at[slot], (o, me))

    def group_copy(c, o, slot):
        return remote(
            gsend.at[part(c)], grecv.at[slot, part(c)], sg.at[c, o], rg.at[c, slot], (o, me)
        )

    upper = jnp.where(rows <= lanes, 1.0, 0.0).astype(bf16)
    copies[0].wait()
    copies[1].wait()
    forget = fg[...]
    logf = jnp.minimum(forget, 0.0) - jnp.log1p(jnp.exp(-jnp.abs(forget)))

    def exact_rows(values, matrix):
        hi, mid, low = split3(values)
        lhs = jnp.concatenate([hi, mid, low, jnp.zeros_like(low)], axis=0)
        out = jnp.dot(lhs, matrix, preferred_element_type=f32)
        n = values.shape[0]
        return out[0:n] + out[n : 2 * n] + out[2 * n : 3 * n]

    cumul = exact_rows(logf, upper)
    level = ig[...] - cumul
    decay = cumul[:, length - 1 : length]
    level_top = jnp.max(level, axis=1, keepdims=True)
    weight = jnp.exp(level - level_top)
    top = decay + level_top

    mine = jnp.where(lane < 64, decay, top)
    pick = lax.div(lax.rem(lane, 64), span) == head_row
    scalars = jnp.sum(jnp.where(pick, mine, 0.0), axis=0, keepdims=True)

    copies[2].wait()
    copies[3].wait()

    def local_state(c):
        for h in range(c * hc, (c + 1) * hc):
            turned = kv[:, h * kd : (h + 1) * kd].astype(f32).T
            scaled = (turned * weight[h : h + 1, :]).astype(bf16)
            state[h] = jnp.dot(scaled, vv[:, h * vd : (h + 1) * vd], preferred_element_type=f32)
        rbuf[me, c * hc : (c + 1) * hc] = slice_of(state, c, me)[...]

    def send_state(c):
        @pl.loop(1, ns)
        def _(d):
            state_copy(c, seq_peer(d), me).start()

    small[...] = scalars
    rsmall[me] = scalars
    local_state(0)
    pl.semaphore_wait(barrier, ns - 1 + ng - 1)

    @pl.loop(1, ns)
    def _(d):
        small_copy(seq_peer(d), me).start()

    send_state(0)
    for c in range(1, CHUNKS):
        local_state(c)
        send_state(c)

    for h in range(heads):
        vector = exact_rows(weight, kv[:, h * kd : (h + 1) * kd])
        vec[h] = vector[h : h + 1, :]
    for h in range(heads):
        @pl.when(me == h * per_head)
        def _(h=h):
            rvec[me] = vec[h]

        @pl.when(me != h * per_head)
        def _(h=h):
            block_vector_copy(h, h * per_head, me).start()

    copies[4].wait()
    columns = []
    for h in range(heads):
        scores = scale * lax.dot_general(
            qv[:, h * kd : (h + 1) * kd], kv[:, h * kd : (h + 1) * kd],
            (((1,), (1,)), ((), ())), preferred_element_type=f32,
        )
        masked = jnp.where(rows >= lanes, level[h : h + 1, :], -jnp.inf)
        reach = jnp.max(masked, axis=1, keepdims=True)
        weighted = jnp.exp(masked - reach) * scores
        inner_den = jnp.sum(weighted, axis=1, keepdims=True)
        cumul_col = jnp.sum(
            jnp.where(rows == lanes, cumul[h : h + 1, :], 0.0), axis=1, keepdims=True
        )
        inner[h] = jnp.dot(
            weighted.astype(bf16), vv[:, h * vd : (h + 1) * vd], preferred_element_type=f32
        )
        columns.append((reach, inner_den, cumul_col))

    @pl.loop(1, ns)
    def _(d):
        o = seq_peer(d)
        small_copy(o, o).wait_recv()

    def widen(out, source):
        for h in range(heads):
            out[h] = jnp.broadcast_to(source[:, h * span : h * span + 1], (ns, 128))

    run_top = jnp.full((1, 128), FLOOR, f32)
    run_dec = jnp.zeros((1, 128), f32)
    for i in range(ns):
        row = rsmall[i]
        top_i = pltpu.roll(row, 64, 1)
        rows_t[i : i + 1, :] = run_top
        rows_d[i : i + 1, :] = run_dec
        early = run_top + row
        joined = jnp.maximum(early, top_i)
        rows_a[i : i + 1, :] = early - joined
        rows_b[i : i + 1, :] = top_i - joined
        run_top = joined
        run_dec = run_dec + row
    lane1 = lax.broadcasted_iota(jnp.int32, (1, 128), 1)
    widen(wide_a, jnp.exp(rows_a[...]))
    widen(wide_b, jnp.exp(rows_b[...]))

    total = jnp.where(lane1 < 64, run_dec, pltpu.roll(run_top, 64, 1))
    gsmall[...] = total
    grsmall[myg] = total

    @pl.loop(myg + 1 if UP else 1, ng)
    def _(d):
        group_small_copy(d if UP else grp_peer(d), myg).start()

    def scan_vector():
        @pl.when(owns_vector)
        def _():
            @pl.loop(1, ns)
            def _(d):
                o = seq_peer(d)
                block_vector_copy(0, o, o).wait_recv()

            run_vec = jnp.zeros((1, 128), f32)
            for i in range(ns):
                nrows[i : i + 1, :] = run_vec
                run_vec = wide_a[myh, i : i + 1, :] * run_vec + wide_b[myh, i : i + 1, :] * rvec[i]
            gvec[...] = run_vec
            grvec[myg] = run_vec

            @pl.loop(myg + 1 if UP else 1, ng)
            def _(d):
                group_vector_copy(d if UP else grp_peer(d), myg).start()

    def scan(c):
        @pl.loop(1, ns)
        def _(d):
            o = seq_peer(d)
            state_copy(c, o, o).wait_recv()

        for h in range(c * hc, (c + 1) * hc):
            run = jnp.zeros((rp, 128), f32)
            for i in range(ns):
                pbuf[i, h] = run
                run = wide_a[h, i : i + 1, :] * run + wide_b[h, i : i + 1, :] * rbuf[i, h]
            gsend[h] = run
        grecv[myg, c * hc : (c + 1) * hc] = gsend[c * hc : (c + 1) * hc]

        @pl.loop(myg + 1 if UP else 1, ng)
        def _(d):
            group_copy(c, d if UP else grp_peer(d), myg).start()

    if ORDER == 0:
        order = [("scan", c) for c in range(CHUNKS)] + [("back", c) for c in range(CHUNKS)]
    else:
        order = [(what, c) for c in range(CHUNKS) for what in ("scan", "back")]
    order = order[:1] + [("group", 0)] + order[1:-1] + [("vector", 0)] + order[-1:] + [("return", 0)]

    found = []

    def before_group():
        @pl.loop(0 if UP else 1, myg if UP else ng)
        def _(d):
            o = d if UP else grp_peer(d)
            group_small_copy(o, o).wait_recv()

        before_top = jnp.full((1, 128), FLOOR, f32)
        for g in range(ng):
            row = grsmall[g]
            top_g = pltpu.roll(row, 64, 1)
            counts = g < myg
            early = before_top + row
            joined = jnp.maximum(early, top_g)
            a = jnp.where(counts, jnp.exp(early - joined), 1.0)
            b = jnp.where(counts, jnp.exp(top_g - joined), 0.0)
            before_top = jnp.where(counts, joined, before_top)
            group_a[g : g + 1, :] = a
            group_b[g : g + 1, :] = b
        tops = rows_t[...]
        early = before_top + rows_d[...]
        full = jnp.maximum(early, tops)
        rows_t[...] = full
        found.append(rows_t[pl.ds(me, 1), :])
        widen(wide_c, jnp.exp(early - full))
        widen(wide_d, jnp.exp(tops - full))
        for h in range(heads):
            group_wide_a[h] = jnp.broadcast_to(group_a[:, h * span : h * span + 1], (ng, 128))
            group_wide_b[h] = jnp.broadcast_to(group_b[:, h * span : h * span + 1], (ng, 128))

    def return_vector():
        @pl.when(owns_vector)
        def _():
            @pl.loop(0 if UP else 1, myg if UP else ng)
            def _(d):
                o = d if UP else grp_peer(d)
                group_vector_copy(o, o).wait_recv()

            before = jnp.zeros((1, 128), f32)
            for g in range(ng):
                before = (
                    group_wide_a[myh, g : g + 1, :] * before
                    + group_wide_b[myh, g : g + 1, :] * grvec[g]
                )
            vectors = wide_c[myh] * before + wide_d[myh] * nrows[...]
            for i in range(ns):
                nback[i] = vectors[i : i + 1, :]
            rnback[myh] = nback[me]

            @pl.loop(1, ns)
            def _(d):
                vector_copy(seq_peer(d), myh).start()

    def back(c):
        @pl.loop(0 if UP else 1, myg if UP else ng)
        def _(d):
            o = d if UP else grp_peer(d)
            group_copy(c, o, o).wait_recv()

        for h in range(c * hc, (c + 1) * hc):
            run = jnp.zeros((rp, 128), f32)
            for g in range(ng):
                run = group_wide_a[h, g : g + 1, :] * run + group_wide_b[h, g : g + 1, :] * grecv[g, h]
            for i in range(ns):
                pbuf[i, h] = wide_c[h, i : i + 1, :] * run + wide_d[h, i : i + 1, :] * pbuf[i, h]

        if BACK == 0:
            @pl.loop(1, ns)
            def _(d):
                back_copy(c, seq_peer(d), me).start()
        else:
            z = lax.rem(me, zdim)

            @pl.loop(0, ns)
            def _(d):
                o = lax.div(d, zdim) * zdim + lax.rem(z + lax.rem(d, zdim), zdim)

                @pl.when(o != me)
                def _():
                    back_copy(c, o, me).start()
        slice_of(pfull, c, me)[...] = pbuf[me, c * hc : (c + 1) * hc]

    for what, c in order:
        if what == "scan":
            scan(c)
        elif what == "back":
            back(c)
        elif what == "group":
            before_group()
        elif what == "vector":
            scan_vector()
        else:
            return_vector()

    for h in range(heads):
        @pl.when(me != h * per_head)
        def _(h=h):
            vector_copy(h * per_head, h).wait_recv()

    for c in range(CHUNKS):
        @pl.loop(1, ns)
        def _(d, c=c):
            o = seq_peer(d)
            back_copy(c, o, o).wait_recv()

        for h in range(c * hc, (c + 1) * hc):
            reach, inner_den, cumul_col = columns[h]
            query = qv[:, h * kd : (h + 1) * kd]
            carried = scale * jnp.dot(query, pfull[h].astype(bf16), preferred_element_type=f32)
            carried_den = scale * jnp.sum(query.astype(f32) * rnback[h], axis=1, keepdims=True)
            prev = found[0][:, h * span : h * span + 1]
            peak = jnp.maximum(prev, reach)
            inner_factor = jnp.exp(reach - peak)
            outer_factor = jnp.exp(prev - peak)
            denom = inner_factor * inner_den + outer_factor * carried_den
            bound = jnp.maximum(jnp.abs(denom), jnp.exp(-(cumul_col + peak)))
            numer = inner_factor * inner[h] + outer_factor * carried
            o_ref[:, h * vd : (h + 1) * vd] = (numer / bound).astype(bf16)

    @pl.loop(1, ns)
    def _(d):
        o = seq_peer(d)
        small_copy(o, me).wait_send()
        for c in range(CHUNKS):
            state_copy(c, o, me).wait_send()
            back_copy(c, o, me).wait_send()

    for h in range(heads):
        @pl.when(me != h * per_head)
        def _(h=h):
            block_vector_copy(h, h * per_head, me).wait_send()

    @pl.when(owns_vector)
    def _():
        @pl.loop(1, ns)
        def _(d):
            vector_copy(seq_peer(d), myh).wait_send()

        @pl.loop(myg + 1 if UP else 1, ng)
        def _(d):
            group_vector_copy(d if UP else grp_peer(d), myg).wait_send()

    @pl.loop(myg + 1 if UP else 1, ng)
    def _(d):
        o = d if UP else grp_peer(d)
        group_small_copy(o, myg).wait_send()
        for c in range(CHUNKS):
            group_copy(c, o, myg).wait_send()


def on_device(ng, ns, queries, key_vectors, value_vectors, input_gate, forget_gate):
    heads, length = input_gate.shape
    kd = queries.shape[1] // heads
    vd = value_vectors.shape[1] // heads
    rp = kd * (vd // 128) // ns
    dma = pltpu.SemaphoreType.DMA

    def wide(*shape):
        return pltpu.VMEM(shape, jnp.float32)

    return pl.pallas_call(
        functools.partial(kernel, ng, ns, heads, kd, vd, length),
        out_shape=jax.ShapeDtypeStruct(value_vectors.shape, jnp.bfloat16),
        in_specs=[pl.BlockSpec(memory_space=pl.ANY)] * 5,
        out_specs=pl.BlockSpec(memory_space=pltpu.VMEM),
        scratch_shapes=[
            wide(heads, length), wide(heads, length),
            pltpu.VMEM(queries.shape, jnp.bfloat16),
            pltpu.VMEM(key_vectors.shape, jnp.bfloat16),
            pltpu.VMEM(value_vectors.shape, jnp.bfloat16),
            wide(heads, kd, vd), wide(heads, length, vd),
            wide(ns, heads, rp, 128), wide(ns, heads, rp, 128), wide(heads, kd, vd),
            wide(heads, rp, 128), wide(ng, heads, rp, 128),
            wide(1, 128), wide(ns, 1, 128), wide(1, 128), wide(ng, 1, 128),
            wide(heads, 1, 128), wide(ns, 1, 128), wide(1, 128), wide(ng, 1, 128),
            wide(ns, 1, 128), wide(heads, 1, 128), wide(ns, 128),
            wide(ns, 128), wide(ns, 128), wide(ns, 128), wide(ns, 128),
            wide(heads, ns, 128), wide(heads, ns, 128), wide(heads, ns, 128), wide(heads, ns, 128),
            wide(ng, 128), wide(ng, 128), wide(heads, ng, 128), wide(heads, ng, 128),
            dma((5,)),
            dma((CHUNKS, ns)), dma((CHUNKS, ns)),
            dma((ns,)), dma((ns,)),
            dma((CHUNKS, ng)), dma((CHUNKS, ng)),
            dma((ng,)), dma((ng,)),
            dma((CHUNKS, ns)), dma((CHUNKS, ns)),
            dma((ns,)), dma((heads,)),
            dma((heads,)), dma((ns,)), dma((ng,)), dma((ng,)),
        ],
        compiler_params=pltpu.CompilerParams(collective_id=0, has_side_effects=True),
        name="mlstm_layer",
    )(queries, key_vectors, value_vectors, input_gate, forget_gate)


def solution(mesh):
    return jax.shard_map(
        functools.partial(on_device, mesh.shape["grp"], mesh.shape["seq"]),
        mesh=mesh,
        in_specs=(
            P(("grp", "seq"), None),
            P(("grp", "seq"), None),
            P(("grp", "seq"), None),
            P(None, ("grp", "seq")),
            P(None, ("grp", "seq")),
        ),
        out_specs=P(("grp", "seq"), None),
        check_vma=False,
    )
```

time: 53.7 us -> 46.3 us (0.86)
  the two profiles are of different devices: /device:TPU:1 before, /device:TPU:30 now
where the time goes in v2:
time: 46.3 us; the launch traced here: 46.2 us
  Pallas kernels  44.5 us (96%)
  local copies, waits for them, and re-layouts  1.67 us (4%)
    pallas_call x1, Pallas kernels, on_device(): pl.pallas_call(functools.partial(kernel, ng, ns, heads, kd, vd, length),...  44.5 us
    unnamed x1, local copies, waits for them, and re-layouts  1.67 us

profile of v2, /device:TPU:30, one launch (start us, length us, event | category | flops | bytes accessed | tf_op | source)
XLA Modules:
  0.0 46.2 jit_solution(10882733062794647272)
XLA Ops:
  0.0 44.5 %mlstm_layer.1 = bf16[128,1024]{1,0:T(8,128)(2,1)} custom-call(bf16[128,512]{1,0:T(8,128)(2,1)} %q_hbm.1, bf16[128,512]{1,0:T(8,128)(2,1)} %k_hbm.1, bf16[128,1024]{1,0:T(8,128)(2,1)} %v_hbm.1, f32[4,128]{1,0:T(4,128)} %ig_hbm.1, f32[4,128]{1,0:T(4,128)} %fg_hbm.1), custom_call_target="tpu_custom_call" | custom-call | tf_op jit(solution)/shard_map/mlstm_layer/pallas_call | solution.py:453
  44.5 1.7 %copy.7 = bf16[128,1024]{1,0:T(8,128)(2,1)} copy(bf16[128,1024]{1,0:T(8,128)(2,1)} %mlstm_layer.1) | data formatting | bytes 524288

commit v3 on v2

--- a/solution.py
+++ b/solution.py
@@ -9,11 +9,8 @@
 
 MESH = pl.DeviceIdType.MESH
 FLOOR = -1e30
-CHUNKS = 2
-BACK = 1
-ORDER = 1
-UP = 1
-EARLY = 1
+SIZES = (2, 2)
+UNROLL = 1
 
 
 def split3(x):
@@ -33,24 +30,33 @@
     in_sem, s1, r1, ss, rs, sg, rg, sgs, rgs, s3, r3, sn, rn, sv, rv, sgv, rgv,
 ):
     f32, bf16 = jnp.float32, jnp.bfloat16
-    hc = heads // CHUNKS
+    chunks = len(SIZES)
+    first = [sum(SIZES[:c]) for c in range(chunks + 1)]
     rp = kd * (vd // 128) // ns
     cols = vd // 128
-    ydim = max(1, ns // 8)
-    zdim = ns // ydim
     per_head = ns // heads
     span = 64 // heads
     scale = kd ** (-0.5)
     myg = lax.axis_index("grp")
     me = lax.axis_index("seq")
-    myh = lax.div(me, per_head)
-    owns_vector = lax.rem(me, per_head) == 0
+    myh = me // per_head
+    owns_vector = (me & (per_head - 1)) == 0
 
     def seq_peer(d):
-        return lax.rem(me + d, ns)
+        return (me + d) & (ns - 1)
 
     def grp_peer(d):
-        return lax.rem(myg + d, ng)
+        return (myg + d) & (ng - 1)
+
+    def each_peer(do):
+        if UNROLL:
+            for d in range(1, ns):
+                do(seq_peer(d))
+        else:
+
+            @pl.loop(1, ns)
+            def _(d):
+                do(seq_peer(d))
 
     copies = [
         pltpu.make_async_copy(src, dst, in_sem.at[n])
@@ -62,21 +68,22 @@
         copy.start()
 
     barrier = pltpu.get_barrier_semaphore()
+
+    def greet(device):
+        pl.semaphore_signal(barrier, inc=1, device_id=device, device_id_type=MESH)
+
+    each_peer(lambda o: greet((myg, o)))
+    for d in range(1, ng):
+        greet((grp_peer(d), me))
+
     zero = jnp.zeros((1, 128), f32)
-    if UP:
-        for g in range(ng):
-            grsmall[g] = zero
-            grvec[g] = zero
-            for h in range(heads):
-                grecv[g, h] = jnp.zeros((rp, 128), f32)
-
-    @pl.loop(1, ns)
-    def _(d):
-        pl.semaphore_signal(barrier, inc=1, device_id=(myg, seq_peer(d)), device_id_type=MESH)
-
-    @pl.loop(1, ng)
-    def _(d):
-        pl.semaphore_signal(barrier, inc=1, device_id=(grp_peer(d), me), device_id_type=MESH)
+
+    @pl.loop(myg + 1, ng)
+    def _(g):
+        grsmall[g] = zero
+        grvec[g] = zero
+        for h in range(heads):
+            grecv[g, h] = jnp.zeros((rp, 128), f32)
 
     lane = lax.broadcasted_iota(jnp.int32, (heads, 128), 1)
     head_row = lax.broadcasted_iota(jnp.int32, (heads, 128), 0)
@@ -84,12 +91,12 @@
     lanes = lax.broadcasted_iota(jnp.int32, (length, length), 1)
 
     def slice_of(ref, c, o):
-        row = pl.multiple_of(lax.div(o, cols) * rp, 8)
-        col = pl.multiple_of(lax.rem(o, cols) * 128, 128)
-        return ref.at[pl.ds(c * hc, hc), pl.ds(row, rp), pl.ds(col, 128)]
+        row = pl.multiple_of((o >> (cols.bit_length() - 1)) * rp, 8)
+        col = pl.multiple_of((o & (cols - 1)) * 128, 128)
+        return ref.at[pl.ds(first[c], SIZES[c]), pl.ds(row, rp), pl.ds(col, 128)]
 
     def part(c):
-        return pl.ds(c * hc, hc)
+        return pl.ds(first[c], SIZES[c])
 
     def remote(src, dst, send, recv, device):
         return pltpu.make_async_remote_copy(
@@ -98,27 +105,46 @@
 
     def small_copy(o, slot):
         return remote(
-            small, rsmall.at[slot], ss.at[o], rs.at[slot], (myg, o)
+            small, rsmall.at[slot], ss.at[0], rs.at[0], (myg, o)
         )
 
     def block_vector_copy(h, o, slot):
-        return remote(vec.at[h], rvec.at[slot], sv.at[h], rv.at[slot], (myg, o))
+        return remote(vec.at[h], rvec.at[slot], sv.at[h], rv.at[0], (myg, o))
 
     def group_vector_copy(o, slot):
         return remote(gvec, grvec.at[slot], sgv.at[o], rgv.at[slot], (o, me))
 
     def state_copy(c, o, slot):
         return remote(
-            slice_of(state, c, o), rbuf.at[slot, part(c)], s1.at[c, o], r1.at[c, slot], (myg, o)
+            slice_of(state, c, o), rbuf.at[slot, part(c)], s1.at[c], r1.at[c], (myg, o)
         )
 
     def back_copy(c, o, slot):
         return remote(
-            pbuf.at[o, part(c)], slice_of(pfull, c, slot), s3.at[c, o], r3.at[c, slot], (myg, o)
+            pbuf.at[o, part(c)], slice_of(pfull, c, slot), s3.at[c], r3.at[c], (myg, o)
         )
 
     def vector_copy(o, h):
-        return remote(nback.at[o], rnback.at[h], sn.at[o], rn.at[h], (myg, o))
+        return remote(nback.at[o], rnback.at[h], sn.at[0], rn.at[h], (myg, o))
+
+    others = pl.ds(0, ns - 1)
+
+    def all_small():
+        return remote(rsmall.at[others], rsmall.at[others], ss.at[0], rs.at[0], (myg, me))
+
+    def all_state(c):
+        ref = rbuf.at[others, part(c)]
+        return remote(ref, ref, s1.at[c], r1.at[c], (myg, me))
+
+    def all_back(c):
+        ref = pbuf.at[others, part(c)]
+        return remote(ref, ref, s3.at[c], r3.at[c], (myg, me))
+
+    def all_block_vectors():
+        return remote(rvec.at[others], rvec.at[others], sv.at[0], rv.at[0], (myg, me))
+
+    def all_vectors():
+        return remote(nback.at[others], nback.at[others], sn.at[0], rn.at[0], (myg, me))
 
     def group_small_copy(o, slot):
         return remote(gsmall, grsmall.at[slot], sgs.at[o], rgs.at[slot], (o, me))
@@ -156,28 +182,24 @@
     copies[3].wait()
 
     def local_state(c):
-        for h in range(c * hc, (c + 1) * hc):
+        for h in range(first[c], first[c + 1]):
             turned = kv[:, h * kd : (h + 1) * kd].astype(f32).T
             scaled = (turned * weight[h : h + 1, :]).astype(bf16)
             state[h] = jnp.dot(scaled, vv[:, h * vd : (h + 1) * vd], preferred_element_type=f32)
-        rbuf[me, c * hc : (c + 1) * hc] = slice_of(state, c, me)[...]
+        rbuf[me, first[c] : first[c + 1]] = slice_of(state, c, me)[...]
 
     def send_state(c):
-        @pl.loop(1, ns)
-        def _(d):
-            state_copy(c, seq_peer(d), me).start()
+        each_peer(lambda o: state_copy(c, o, me).start())
 
     small[...] = scalars
     rsmall[me] = scalars
     local_state(0)
     pl.semaphore_wait(barrier, ns - 1 + ng - 1)
 
-    @pl.loop(1, ns)
-    def _(d):
-        small_copy(seq_peer(d), me).start()
+    each_peer(lambda o: small_copy(o, me).start())
 
     send_state(0)
-    for c in range(1, CHUNKS):
+    for c in range(1, chunks):
         local_state(c)
         send_state(c)
 
@@ -212,10 +234,7 @@
         )
         columns.append((reach, inner_den, cumul_col))
 
-    @pl.loop(1, ns)
-    def _(d):
-        o = seq_peer(d)
-        small_copy(o, o).wait_recv()
+    all_small().wait_recv()
 
     def widen(out, source):
         for h in range(heads):
@@ -242,17 +261,14 @@
     gsmall[...] = total
     grsmall[myg] = total
 
-    @pl.loop(myg + 1 if UP else 1, ng)
+    @pl.loop(myg + 1, ng)
     def _(d):
-        group_small_copy(d if UP else grp_peer(d), myg).start()
+        group_small_copy(d, myg).start()
 
     def scan_vector():
         @pl.when(owns_vector)
         def _():
-            @pl.loop(1, ns)
-            def _(d):
-                o = seq_peer(d)
-                block_vector_copy(0, o, o).wait_recv()
+            all_block_vectors().wait_recv()
 
             run_vec = jnp.zeros((1, 128), f32)
             for i in range(ns):
@@ -261,40 +277,34 @@
             gvec[...] = run_vec
             grvec[myg] = run_vec
 
-            @pl.loop(myg + 1 if UP else 1, ng)
+            @pl.loop(myg + 1, ng)
             def _(d):
-                group_vector_copy(d if UP else grp_peer(d), myg).start()
+                group_vector_copy(d, myg).start()
 
     def scan(c):
-        @pl.loop(1, ns)
-        def _(d):
-            o = seq_peer(d)
-            state_copy(c, o, o).wait_recv()
-
-        for h in range(c * hc, (c + 1) * hc):
+        all_state(c).wait_recv()
+
+        for h in range(first[c], first[c + 1]):
             run = jnp.zeros((rp, 128), f32)
             for i in range(ns):
                 pbuf[i, h] = run
                 run = wide_a[h, i : i + 1, :] * run + wide_b[h, i : i + 1, :] * rbuf[i, h]
             gsend[h] = run
-        grecv[myg, c * hc : (c + 1) * hc] = gsend[c * hc : (c + 1) * hc]
-
-        @pl.loop(myg + 1 if UP else 1, ng)
+        grecv[myg, first[c] : first[c + 1]] = gsend[first[c] : first[c + 1]]
+
+        @pl.loop(myg + 1, ng)
         def _(d):
-            group_copy(c, d if UP else grp_peer(d), myg).start()
-
-    if ORDER == 0:
-        order = [("scan", c) for c in range(CHUNKS)] + [("back", c) for c in range(CHUNKS)]
-    else:
-        order = [(what, c) for c in range(CHUNKS) for what in ("scan", "back")]
+            group_copy(c, d, myg).start()
+
+    order = [(what, c) for c in range(chunks) for what in ("scan", "back")]
     order = order[:1] + [("group", 0)] + order[1:-1] + [("vector", 0)] + order[-1:] + [("return", 0)]
 
     found = []
 
     def before_group():
-        @pl.loop(0 if UP else 1, myg if UP else ng)
+        @pl.loop(0, myg)
         def _(d):
-            o = d if UP else grp_peer(d)
+            o = d
             group_small_copy(o, o).wait_recv()
 
         before_top = jnp.full((1, 128), FLOOR, f32)
@@ -323,9 +333,9 @@
     def return_vector():
         @pl.when(owns_vector)
         def _():
-            @pl.loop(0 if UP else 1, myg if UP else ng)
+            @pl.loop(0, myg)
             def _(d):
-                o = d if UP else grp_peer(d)
+                o = d
                 group_vector_copy(o, o).wait_recv()
 
             before = jnp.zeros((1, 128), f32)
@@ -344,33 +354,20 @@
                 vector_copy(seq_peer(d), myh).start()
 
     def back(c):
-        @pl.loop(0 if UP else 1, myg if UP else ng)
+        @pl.loop(0, myg)
         def _(d):
-            o = d if UP else grp_peer(d)
+            o = d
             group_copy(c, o, o).wait_recv()
 
-        for h in range(c * hc, (c + 1) * hc):
+        for h in range(first[c], first[c + 1]):
             run = jnp.zeros((rp, 128), f32)
             for g in range(ng):
                 run = group_wide_a[h, g : g + 1, :] * run + group_wide_b[h, g : g + 1, :] * grecv[g, h]
             for i in range(ns):
                 pbuf[i, h] = wide_c[h, i : i + 1, :] * run + wide_d[h, i : i + 1, :] * pbuf[i, h]
 
-        if BACK == 0:
-            @pl.loop(1, ns)
-            def _(d):
-                back_copy(c, seq_peer(d), me).start()
-        else:
-            z = lax.rem(me, zdim)
-
-            @pl.loop(0, ns)
-            def _(d):
-                o = lax.div(d, zdim) * zdim + lax.rem(z + lax.rem(d, zdim), zdim)
-
-                @pl.when(o != me)
-                def _():
-                    back_copy(c, o, me).start()
-        slice_of(pfull, c, me)[...] = pbuf[me, c * hc : (c + 1) * hc]
+        each_peer(lambda o: back_copy(c, o, me).start())
+        slice_of(pfull, c, me)[...] = pbuf[me, first[c] : first[c + 1]]
 
     for what, c in order:
         if what == "scan":
@@ -389,13 +386,10 @@
         def _(h=h):
             vector_copy(h * per_head, h).wait_recv()
 
-    for c in range(CHUNKS):
-        @pl.loop(1, ns)
-        def _(d, c=c):
-            o = seq_peer(d)
-            back_copy(c, o, o).wait_recv()
-
-        for h in range(c * hc, (c + 1) * hc):
+    for c in range(chunks):
+        all_back(c).wait_recv()
+
+        for h in range(first[c], first[c + 1]):
             reach, inner_den, cumul_col = columns[h]
             query = qv[:, h * kd : (h + 1) * kd]
             carried = scale * jnp.dot(query, pfull[h].astype(bf16), preferred_element_type=f32)
@@ -409,13 +403,10 @@
             numer = inner_factor * inner[h] + outer_factor * carried
             o_ref[:, h * vd : (h + 1) * vd] = (numer / bound).astype(bf16)
 
-    @pl.loop(1, ns)
-    def _(d):
-        o = seq_peer(d)
-        small_copy(o, me).wait_send()
-        for c in range(CHUNKS):
-            state_copy(c, o, me).wait_send()
-            back_copy(c, o, me).wait_send()
+    all_small().wait_send()
+    for c in range(chunks):
+        all_state(c).wait_send()
+        all_back(c).wait_send()
 
     for h in range(heads):
         @pl.when(me != h * per_head)
@@ -424,19 +415,17 @@
 
     @pl.when(owns_vector)
     def _():
-        @pl.loop(1, ns)
+        all_vectors().wait_send()
+
+        @pl.loop(myg + 1, ng)
         def _(d):
-            vector_copy(seq_peer(d), myh).wait_send()
-
-        @pl.loop(myg + 1 if UP else 1, ng)
-        def _(d):
-            group_vector_copy(d if UP else grp_peer(d), myg).wait_send()
-
-    @pl.loop(myg + 1 if UP else 1, ng)
+            group_vector_copy(d, myg).wait_send()
+
+    @pl.loop(myg + 1, ng)
     def _(d):
-        o = d if UP else grp_peer(d)
+        o = d
         group_small_copy(o, myg).wait_send()
-        for c in range(CHUNKS):
+        for c in range(chunks):
             group_copy(c, o, myg).wait_send()
 
 
@@ -452,7 +441,7 @@
 
     return pl.pallas_call(
         functools.partial(kernel, ng, ns, heads, kd, vd, length),
-        out_shape=jax.ShapeDtypeStruct(value_vectors.shape, jnp.bfloat16),
+        out_shape=pltpu.VMEM(value_vectors.shape, jnp.bfloat16),
         in_specs=[pl.BlockSpec(memory_space=pl.ANY)] * 5,
         out_specs=pl.BlockSpec(memory_space=pltpu.VMEM),
         scratch_shapes=[
@@ -470,13 +459,10 @@
             wide(heads, ns, 128), wide(heads, ns, 128), wide(heads, ns, 128), wide(heads, ns, 128),
             wide(ng, 128), wide(ng, 128), wide(heads, ng, 128), wide(heads, ng, 128),
             dma((5,)),
-            dma((CHUNKS, ns)), dma((CHUNKS, ns)),
-            dma((ns,)), dma((ns,)),
-            dma((CHUNKS, ng)), dma((CHUNKS, ng)),
-            dma((ng,)), dma((ng,)),
-            dma((CHUNKS, ns)), dma((CHUNKS, ns)),
-            dma((ns,)), dma((heads,)),
-            dma((heads,)), dma((ns,)), dma((ng,)), dma((ng,)),
+            dma((len(SIZES),)), dma((len(SIZES),)), dma((1,)), dma((1,)),
+            dma((len(SIZES), ng)), dma((len(SIZES), ng)), dma((ng,)), dma((ng,)),
+            dma((len(SIZES),)), dma((len(SIZES),)), dma((1,)), dma((heads,)),
+            dma((heads,)), dma((1,)), dma((ng,)), dma((ng,)),
         ],
         compiler_params=pltpu.CompilerParams(collective_id=0, has_side_effects=True),
         name="mlstm_layer",

time: 46.3 us -> 40.3 us (0.87)
  Pallas kernels: 44.5 us -> 39.5 us
  local copies, waits for them, and re-layouts: 1.67 us -> 0.71 us
    pallas_call x1, Pallas kernels: 44.5 us -> 39.5 us  [on_device(): pl.pallas_call(functools.partial(kernel, ng, ns, heads, kd, vd, length),...]
    unnamed x1, local copies, waits for them, and re-layouts: 1.67 us -> 0.71 us
where the time goes in v3:
time: 40.3 us; the launch traced here: 40.2 us
  Pallas kernels  39.5 us (98%)
  local copies, waits for them, and re-layouts  0.71 us (2%)
    pallas_call x1, Pallas kernels, on_device(): pl.pallas_call(functools.partial(kernel, ng, ns, heads, kd, vd, length),...  39.5 us

profile of v3, /device:TPU:30, one launch (start us, length us, event | category | flops | bytes accessed | tf_op | source)
XLA Modules:
  0.0 40.2 jit_solution(3805901464340481930)
XLA Ops:
  0.0 39.5 %mlstm_layer.1 = bf16[128,1024]{1,0:T(8,128)(2,1)S(1)} custom-call(bf16[128,512]{1,0:T(8,128)(2,1)} %q_hbm.1, bf16[128,512]{1,0:T(8,128)(2,1)} %k_hbm.1, bf16[128,1024]{1,0:T(8,128)(2,1)} %v_hbm.1, f32[4,128]{1,0:T(4,128)} %ig_hbm.1, f32[4,128]{1,0:T(4,128)} %fg_hbm.1), custom_call_target="tpu_custom_call" | custom-call | tf_op jit(solution)/shard_map/mlstm_layer/pallas_call | solution.py:442
  39.5 0.7 %copy.7 = bf16[128,1024]{1,0:T(8,128)(2,1)} copy(bf16[128,1024]{1,0:T(8,128)(2,1)S(1)} %mlstm_layer.1) | data formatting | bytes 524288

commit v4 on v3

--- a/solution.py
+++ b/solution.py
@@ -10,7 +10,7 @@
 MESH = pl.DeviceIdType.MESH
 FLOOR = -1e30
 SIZES = (2, 2)
-UNROLL = 1
+COLUMNS = (0, 1, 2, 3, 4, 7, 5, 6)
 
 
 def split3(x):
@@ -48,15 +48,32 @@
     def grp_peer(d):
         return (myg + d) & (ng - 1)
 
+    zdim = min(8, ns)
+    ydim = ns // zdim
+    zbits = zdim.bit_length() - 1
+    y, z = me >> zbits, me & (zdim - 1)
+
     def each_peer(do):
-        if UNROLL:
-            for d in range(1, ns):
-                do(seq_peer(d))
-        else:
-
-            @pl.loop(1, ns)
-            def _(d):
-                do(seq_peer(d))
+        for d in range(1, ns):
+            do(seq_peer(d))
+
+    def far_first(do):
+        def far(n, size):
+            return min(n, size - n)
+
+        steps = [(dy, dz) for dy in range(ydim) for dz in range(zdim) if dy or dz]
+        steps.sort(key=lambda t: (far(t[1], zdim), far(t[0], ydim)), reverse=True)
+        for dy, dz in steps:
+            do((((y + dy) & (ydim - 1)) << zbits) | ((z + dz) & (zdim - 1)))
+
+    def to_columns(do, columns):
+        for to in columns:
+            for dy in range(ydim):
+                o = (((y + dy) & (ydim - 1)) << zbits) | to
+                if dy:
+                    do(o)
+                else:
+                    pl.when(to != z)(functools.partial(do, o))
 
     copies = [
         pltpu.make_async_copy(src, dst, in_sem.at[n])
@@ -189,7 +206,7 @@
         rbuf[me, first[c] : first[c + 1]] = slice_of(state, c, me)[...]
 
     def send_state(c):
-        each_peer(lambda o: state_copy(c, o, me).start())
+        far_first(lambda o: state_copy(c, o, me).start())
 
     small[...] = scalars
     rsmall[me] = scalars
@@ -366,7 +383,7 @@
             for i in range(ns):
                 pbuf[i, h] = wide_c[h, i : i + 1, :] * run + wide_d[h, i : i + 1, :] * pbuf[i, h]
 
-        each_peer(lambda o: back_copy(c, o, me).start())
+        to_columns(lambda o: back_copy(c, o, me).start(), COLUMNS)
         slice_of(pfull, c, me)[...] = pbuf[me, first[c] : first[c + 1]]
 
     for what, c in order:

time: 40.3 us -> 38.9 us (0.965)
  the two profiles are of different devices: /device:TPU:30 before, /device:TPU:70 now
where the time goes in v4:
time: 38.9 us; the launch traced here: 38.8 us
  Pallas kernels  38.1 us (98%)
  local copies, waits for them, and re-layouts  0.71 us (2%)
    pallas_call x1, Pallas kernels, on_device(): pl.pallas_call(functools.partial(kernel, ng, ns, heads, kd, vd, length),...  38.1 us

profile of v4, /device:TPU:70, one launch (start us, length us, event | category | flops | bytes accessed | tf_op | source)
XLA Modules:
  0.0 38.8 jit_solution(9927183521865651968)
XLA Ops:
  0.0 38.1 %mlstm_layer.1 = bf16[128,1024]{1,0:T(8,128)(2,1)S(1)} custom-call(bf16[128,512]{1,0:T(8,128)(2,1)} %q_hbm.1, bf16[128,512]{1,0:T(8,128)(2,1)} %k_hbm.1, bf16[128,1024]{1,0:T(8,128)(2,1)} %v_hbm.1, f32[4,128]{1,0:T(4,128)} %ig_hbm.1, f32[4,128]{1,0:T(4,128)} %fg_hbm.1), custom_call_target="tpu_custom_call" | custom-call | tf_op jit(solution)/shard_map/mlstm_layer/pallas_call | solution.py:459
  38.1 0.7 %copy.7 = bf16[128,1024]{1,0:T(8,128)(2,1)} copy(bf16[128,1024]{1,0:T(8,128)(2,1)S(1)} %mlstm_layer.1) | data formatting | bytes 524288

commit v5 on v4

--- a/solution.py
+++ b/solution.py
@@ -9,7 +9,7 @@
 
 MESH = pl.DeviceIdType.MESH
 FLOOR = -1e30
-SIZES = (2, 2)
+SIZES = (1, 1, 1, 1)
 COLUMNS = (0, 1, 2, 3, 4, 7, 5, 6)
 
 

time: 38.9 us -> 37.6 us (0.967)
  the two profiles are of different devices: /device:TPU:70 before, /device:TPU:32 now
where the time goes in v5:
time: 37.6 us; the launch traced here: 37.5 us
  Pallas kernels  36.8 us (98%)
  local copies, waits for them, and re-layouts  0.71 us (2%)
    pallas_call x1, Pallas kernels, on_device(): pl.pallas_call(functools.partial(kernel, ng, ns, heads, kd, vd, length),...  36.8 us

profile of v5, /device:TPU:32, one launch (start us, length us, event | category | flops | bytes accessed | tf_op | source)
XLA Modules:
  0.0 37.5 jit_solution(855595424710078659)
XLA Ops:
  0.0 36.8 %mlstm_layer.1 = bf16[128,1024]{1,0:T(8,128)(2,1)S(1)} custom-call(bf16[128,512]{1,0:T(8,128)(2,1)} %q_hbm.1, bf16[128,512]{1,0:T(8,128)(2,1)} %k_hbm.1, bf16[128,1024]{1,0:T(8,128)(2,1)} %v_hbm.1, f32[4,128]{1,0:T(4,128)} %ig_hbm.1, f32[4,128]{1,0:T(4,128)} %fg_hbm.1), custom_call_target="tpu_custom_call" | custom-call | tf_op jit(solution)/shard_map/mlstm_layer/pallas_call | solution.py:459
  36.8 0.7 %copy.7 = bf16[128,1024]{1,0:T(8,128)(2,1)} copy(bf16[128,1024]{1,0:T(8,128)(2,1)S(1)} %mlstm_layer.1) | data formatting | bytes 524288

commit v6 on v5

--- a/solution.py
+++ b/solution.py
@@ -67,13 +67,11 @@
             do((((y + dy) & (ydim - 1)) << zbits) | ((z + dz) & (zdim - 1)))
 
     def to_columns(do, columns):
-        for to in columns:
-            for dy in range(ydim):
-                o = (((y + dy) & (ydim - 1)) << zbits) | to
-                if dy:
-                    do(o)
-                else:
-                    pl.when(to != z)(functools.partial(do, o))
+        for low in range(0, ydim, 2):
+            for to in columns:
+                for k in range(min(2, ydim)):
+                    o = ((low + ((y + k) & (min(2, ydim) - 1))) << zbits) | to
+                    pl.when(o != me)(functools.partial(do, o))
 
     copies = [
         pltpu.make_async_copy(src, dst, in_sem.at[n])

time: 37.6 us -> 37.1 us (0.987)
  Pallas kernels: 36.8 us -> 36.3 us
    pallas_call x1, Pallas kernels: 36.8 us -> 36.3 us  [on_device(): pl.pallas_call(functools.partial(kernel, ng, ns, heads, kd, vd, length),...]
where the time goes in v6:
time: 37.1 us
  Pallas kernels  36.3 us (98%)
  local copies, waits for them, and re-layouts  0.71 us (2%)
    pallas_call x1, Pallas kernels, on_device(): pl.pallas_call(functools.partial(kernel, ng, ns, heads, kd, vd, length),...  36.3 us

profile of v6, /device:TPU:32, one launch (start us, length us, event | category | flops | bytes accessed | tf_op | source)
XLA Modules:
  0.0 37.1 jit_solution(15513596183058763372)
XLA Ops:
  0.0 36.3 %mlstm_layer.1 = bf16[128,1024]{1,0:T(8,128)(2,1)S(1)} custom-call(bf16[128,512]{1,0:T(8,128)(2,1)} %q_hbm.1, bf16[128,512]{1,0:T(8,128)(2,1)} %k_hbm.1, bf16[128,1024]{1,0:T(8,128)(2,1)} %v_hbm.1, f32[4,128]{1,0:T(4,128)} %ig_hbm.1, f32[4,128]{1,0:T(4,128)} %fg_hbm.1), custom_call_target="tpu_custom_call" | custom-call | tf_op jit(solution)/shard_map/mlstm_layer/pallas_call | solution.py:457
  36.3 0.7 %copy.7 = bf16[128,1024]{1,0:T(8,128)(2,1)} copy(bf16[128,1024]{1,0:T(8,128)(2,1)S(1)} %mlstm_layer.1) | data formatting | bytes 524288

commit v7 on v6

--- a/solution.py
+++ b/solution.py
@@ -10,6 +10,7 @@
 MESH = pl.DeviceIdType.MESH
 FLOOR = -1e30
 SIZES = (1, 1, 1, 1)
+RET = 6
 COLUMNS = (0, 1, 2, 3, 4, 7, 5, 6)
 
 
@@ -40,7 +41,8 @@
     myg = lax.axis_index("grp")
     me = lax.axis_index("seq")
     myh = me // per_head
-    owns_vector = (me & (per_head - 1)) == 0
+    keeper = 0
+    owns_vector = (me & (per_head - 1)) == keeper
 
     def seq_peer(d):
         return (me + d) & (ns - 1)
@@ -62,7 +64,7 @@
             return min(n, size - n)
 
         steps = [(dy, dz) for dy in range(ydim) for dz in range(zdim) if dy or dz]
-        steps.sort(key=lambda t: (far(t[1], zdim), far(t[0], ydim)), reverse=True)
+        steps.sort(key=lambda t: (far(t[0], ydim) + far(t[1], zdim)), reverse=True)
         for dy, dz in steps:
             do((((y + dy) & (ydim - 1)) << zbits) | ((z + dz) & (zdim - 1)))
 
@@ -214,21 +216,21 @@
     each_peer(lambda o: small_copy(o, me).start())
 
     send_state(0)
-    for c in range(1, chunks):
-        local_state(c)
-        send_state(c)
-
     for h in range(heads):
         vector = exact_rows(weight, kv[:, h * kd : (h + 1) * kd])
         vec[h] = vector[h : h + 1, :]
     for h in range(heads):
-        @pl.when(me == h * per_head)
+        @pl.when(me == h * per_head + keeper)
         def _(h=h):
             rvec[me] = vec[h]
 
-        @pl.when(me != h * per_head)
+        @pl.when(me != h * per_head + keeper)
         def _(h=h):
-            block_vector_copy(h, h * per_head, me).start()
+            block_vector_copy(h, h * per_head + keeper, me).start()
+
+    for c in range(1, chunks):
+        local_state(c)
+        send_state(c)
 
     copies[4].wait()
     columns = []
@@ -312,7 +314,9 @@
             group_copy(c, d, myg).start()
 
     order = [(what, c) for c in range(chunks) for what in ("scan", "back")]
-    order = order[:1] + [("group", 0)] + order[1:-1] + [("vector", 0)] + order[-1:] + [("return", 0)]
+    order = (
+        order[:1] + [("group", 0)] + order[1:2] + [("vector", 0)] + order[2:RET] + [("return", 0)] + order[RET:]
+    )
 
     found = []
 
@@ -396,10 +400,30 @@
         else:
             return_vector()
 
+    all_small().wait_send()
+    for c in range(chunks):
+        all_state(c).wait_send()
     for h in range(heads):
-        @pl.when(me != h * per_head)
+        @pl.when(me != h * per_head + keeper)
         def _(h=h):
-            vector_copy(h * per_head, h).wait_recv()
+            block_vector_copy(h, h * per_head + keeper, me).wait_send()
+
+    @pl.when(owns_vector)
+    def _():
+        @pl.loop(myg + 1, ng)
+        def _(d):
+            group_vector_copy(d, myg).wait_send()
+
+    @pl.loop(myg + 1, ng)
+    def _(d):
+        group_small_copy(d, myg).wait_send()
+        for c in range(chunks):
+            group_copy(c, d, myg).wait_send()
+
+    for h in range(heads):
+        @pl.when(me != h * per_head + keeper)
+        def _(h=h):
+            vector_copy(h * per_head + keeper, h).wait_recv()
 
     for c in range(chunks):
         all_back(c).wait_recv()
@@ -418,30 +442,12 @@
             numer = inner_factor * inner[h] + outer_factor * carried
             o_ref[:, h * vd : (h + 1) * vd] = (numer / bound).astype(bf16)
 
-    all_small().wait_send()
     for c in range(chunks):
-        all_state(c).wait_send()
         all_back(c).wait_send()
-
-    for h in range(heads):
-        @pl.when(me != h * per_head)
-        def _(h=h):
-            block_vector_copy(h, h * per_head, me).wait_send()
 
     @pl.when(owns_vector)
     def _():
         all_vectors().wait_send()
-
-        @pl.loop(myg + 1, ng)
-        def _(d):
-            group_vector_copy(d, myg).wait_send()
-
-    @pl.loop(myg + 1, ng)
-    def _(d):
-        o = d
-        group_small_copy(o, myg).wait_send()
-        for c in range(chunks):
-            group_copy(c, o, myg).wait_send()
 
 
 def on_device(ng, ns, queries, key_vectors, value_vectors, input_gate, forget_gate):

time: 37.1 us -> 36.9 us (level)
  no operation moved by 1% of the time
where the time goes in v7:
time: 36.9 us; the launch traced here: 36.8 us
  Pallas kernels  36.1 us (98%)
  local copies, waits for them, and re-layouts  0.71 us (2%)
    pallas_call x1, Pallas kernels, on_device(): pl.pallas_call(functools.partial(kernel, ng, ns, heads, kd, vd, length),...  36.1 us

profile of v7, /device:TPU:32, one launch (start us, length us, event | category | flops | bytes accessed | tf_op | source)
XLA Modules:
  0.0 36.8 jit_solution(1410396143050485691)
XLA Ops:
  0.0 36.1 %mlstm_layer.1 = bf16[128,1024]{1,0:T(8,128)(2,1)S(1)} custom-call(bf16[128,512]{1,0:T(8,128)(2,1)} %q_hbm.1, bf16[128,512]{1,0:T(8,128)(2,1)} %k_hbm.1, bf16[128,1024]{1,0:T(8,128)(2,1)} %v_hbm.1, f32[4,128]{1,0:T(4,128)} %ig_hbm.1, f32[4,128]{1,0:T(4,128)} %fg_hbm.1), custom_call_target="tpu_custom_call" | custom-call | tf_op jit(solution)/shard_map/mlstm_layer/pallas_call | solution.py:463
  36.1 0.7 %copy.7 = bf16[128,1024]{1,0:T(8,128)(2,1)} copy(bf16[128,1024]{1,0:T(8,128)(2,1)S(1)} %mlstm_layer.1) | data formatting | bytes 524288

commit v8 on v7

--- a/solution.py
+++ b/solution.py
@@ -210,7 +210,8 @@
 
     small[...] = scalars
     rsmall[me] = scalars
-    local_state(0)
+    for c in range(chunks):
+        local_state(c)
     pl.semaphore_wait(barrier, ns - 1 + ng - 1)
 
     each_peer(lambda o: small_copy(o, me).start())
@@ -229,7 +230,6 @@
             block_vector_copy(h, h * per_head + keeper, me).start()
 
     for c in range(1, chunks):
-        local_state(c)
         send_state(c)
 
     copies[4].wait()

time: 36.9 us -> 36.9 us (level)
  no operation moved by 1% of the time
where the time goes in v8:
time: 36.9 us; the launch traced here: 36.8 us
  Pallas kernels  36.1 us (98%)
  local copies, waits for them, and re-layouts  0.71 us (2%)
    pallas_call x1, Pallas kernels, on_device(): pl.pallas_call(functools.partial(kernel, ng, ns, heads, kd, vd, length),...  36.1 us

profile of v8, /device:TPU:32, one launch (start us, length us, event | category | flops | bytes accessed | tf_op | source)
XLA Modules:
  0.0 36.8 jit_solution(14144447921926614163)
XLA Ops:
  0.0 36.1 %mlstm_layer.1 = bf16[128,1024]{1,0:T(8,128)(2,1)S(1)} custom-call(bf16[128,512]{1,0:T(8,128)(2,1)} %q_hbm.1, bf16[128,512]{1,0:T(8,128)(2,1)} %k_hbm.1, bf16[128,1024]{1,0:T(8,128)(2,1)} %v_hbm.1, f32[4,128]{1,0:T(4,128)} %ig_hbm.1, f32[4,128]{1,0:T(4,128)} %fg_hbm.1), custom_call_target="tpu_custom_call" | custom-call | tf_op jit(solution)/shard_map/mlstm_layer/pallas_call | solution.py:463
  36.1 0.7 %copy.7 = bf16[128,1024]{1,0:T(8,128)(2,1)} copy(bf16[128,1024]{1,0:T(8,128)(2,1)S(1)} %mlstm_layer.1) | data formatting | bytes 524288
